TPU v7x, 32 devices: a whole 2x2x4 slice. The times are simulated.
32 devices in a mesh: row: 4 (over x, core), col: 8 (over z, y).
Axes of the slice: x: 2, y: 2, z: 4, core: 2. Of those that a mesh axis runs over, the one named last changes fastest.
Arguments:
- front_panels: float32 [16, 4, 256, 8, 8, 256], P(None, 'row', 'col'), as said below
- child_update_tiles: float32 [4, 8, 8, 256, 256], P('row', 'col'), may hold values from -2 to 2
- child_rows: int32 [4, 8, 8], P('row', 'col'), may hold values from 0 to 63, as said below
- child_cols: int32 [4, 8, 8], P('row', 'col'), may hold values from 0 to 7
- child_counts: int32 [4, 8], P('row', 'col'), may hold values from 4 to 8, as said below
- row_maps: int32 [4, 8, 8, 256], P('row', 'col'), may hold values from 0 to 255, each once within a row
- col_maps: int32 [4, 8, 8, 256], P('row', 'col'), may hold values from 0 to 255, each once within a row
Outputs:
- factored_front: float32 [16, 4, 256, 8, 8, 256], P(None, 'row', None, None, 'col')
Inputs may be any that keep to these rules, and one draw needn't show every extreme that they name: child_rows[r, c, k] modulo 4 names one of four owner rows; among the live slots of one device at most 2 name the same owner row, and some device sends exactly 2 to some owner; every slot's target tile column is at most its target tile row. `child_counts`: every device of col index 0 has all slots live. `front_panels`: the diagonal of the front dominates its first tile, so that tile stays positive definite after the children are added.
All inputs are finite; a program needn't handle non-finite values.
Results may differ from a plain program's by a relative error of at most 0.0003.
Values sent between devices are 32-bit elements; how exact they have to be, the bound alone decides.
No kernel may reach another device: no remote copies, remote signals or barrier semaphores. Data moves between devices by JAX's collectives and lax.ppermute only.
A program may use at most 320 MiB of HBM per device.

v0:
```python
import jax
import jax.numpy as jnp
from jax import lax
from jax.sharding import PartitionSpec as P


def broadcast(value, axis, source):
    kept = jnp.where(lax.axis_index(axis) == source, value, 0).astype(value.dtype)
    return lax.psum(kept, axis)


def slot_positions(owners, is_live):
    slot_entries = owners.shape[-1]
    earlier = lax.broadcasted_iota(
        jnp.int32, (slot_entries, slot_entries), 0
    ) < lax.broadcasted_iota(jnp.int32, (slot_entries, slot_entries), 1)
    same_owner = (owners[..., :, None] == owners[..., None, :]) & is_live[..., :, None] & earlier
    return jnp.sum(same_owner.astype(jnp.int32), axis=-2)


def on_device(
    front_panels, child_update_tiles, child_rows, child_cols, child_counts, row_maps, col_maps
):
    largest_index = lax.Precision.HIGHEST
    row_size = lax.axis_size("row")
    col_size = lax.axis_size("col")
    my_row = lax.axis_index("row")
    my_col = lax.axis_index("col")
    front_width = front_panels.shape[-1]
    blocks = lax.all_to_all(front_panels, "col", split_axis=4, concat_axis=2, tiled=True)
    row_tiles = blocks.shape[0]
    col_tiles = blocks.shape[3]
    blocks = blocks.reshape(row_tiles, front_width, col_tiles, front_width)
    slot_entries = child_update_tiles.shape[2]
    capacity = slot_entries // 4
    labels = lax.broadcasted_iota(jnp.int32, (1, 1, front_width), 2)
    row_indicator = (row_maps.reshape(slot_entries, front_width)[:, :, None] == labels).astype(
        jnp.float32
    )
    column_indicator = (col_maps.reshape(slot_entries, front_width)[:, :, None] == labels).astype(
        jnp.float32
    )
    shifted_tiles = jnp.einsum(
        "gml,gmq->glq",
        row_indicator,
        child_update_tiles.reshape(slot_entries, front_width, front_width),
        precision=largest_index,
    )
    shifted_tiles = jnp.einsum(
        "afb,abx->afx", shifted_tiles, column_indicator, precision=largest_index
    )
    slot_ids = lax.broadcasted_iota(jnp.int32, (slot_entries,), 0)
    is_live = slot_ids < child_counts.reshape(())
    owners = child_rows.reshape(slot_entries) % row_size
    positions = slot_positions(owners, is_live)
    dest_ids = lax.broadcasted_iota(jnp.int32, (row_size, capacity, slot_entries), 0)
    place_ids = lax.broadcasted_iota(jnp.int32, (row_size, capacity, slot_entries), 1)
    selector = (
        (owners[None, None, :] == dest_ids)
        & (positions[None, None, :] == place_ids)
        & is_live[None, None, :]
    ).astype(jnp.float32)
    outgoing = jnp.einsum(
        "opk,kx->opx",
        selector,
        shifted_tiles.reshape(slot_entries, front_width * front_width),
        precision=largest_index,
    )
    incoming = lax.all_to_all(outgoing, "row", split_axis=0, concat_axis=0, tiled=True)
    all_rows, all_cols, all_counts = (
        lax.all_gather(child_rows, "row", axis=0, tiled=True),
        lax.all_gather(child_cols, "row", axis=0, tiled=True),
        lax.all_gather(child_counts, "row", axis=0, tiled=True),
    )
    source_rows = all_rows.reshape(row_size, slot_entries)
    source_cols = all_cols.reshape(row_size, slot_entries)
    source_live = slot_ids[None, :] < all_counts.reshape(row_size)[:, None]
    source_owner = source_rows % row_size
    source_pos = slot_positions(source_owner, source_live)
    mine = (source_live & (source_owner == my_row)).astype(jnp.float32)
    depth_onehot = (
        (source_rows // row_size)[:, :, None]
        == lax.broadcasted_iota(jnp.int32, (1, 1, row_tiles), 2)
    ).astype(jnp.float32) * mine[:, :, None]
    across_onehot = (
        source_cols[:, :, None] == lax.broadcasted_iota(jnp.int32, (1, 1, col_tiles), 2)
    ).astype(jnp.float32)
    place_onehot = (
        source_pos[:, :, None] == lax.broadcasted_iota(jnp.int32, (1, 1, capacity), 2)
    ).astype(jnp.float32)
    landing = jnp.einsum(
        "ska,skb,skp->absp", depth_onehot, across_onehot, place_onehot, precision=largest_index
    )
    incoming = incoming.reshape(row_size, capacity, front_width, front_width)
    blocks = blocks + jnp.einsum("absp,spxy->axby", landing, incoming, precision=largest_index)
    tile_i = lax.broadcasted_iota(jnp.int32, (row_tiles, 1, col_tiles, 1), 0) * row_size + my_row
    tile_j = lax.broadcasted_iota(jnp.int32, (row_tiles, 1, col_tiles, 1), 2) * col_size + my_col
    flipped = jnp.einsum("axby->aybx", blocks)
    blocks = jnp.where(tile_i == tile_j, 0.5 * (blocks + flipped), blocks)
    identity = jnp.eye(front_width, dtype=jnp.float32)
    corner = blocks[0, :, 0, :]
    at_root = (my_row == 0) & (my_col == 0)
    factor = jnp.linalg.cholesky(jnp.where(at_root, corner, identity))
    factor = broadcast(factor, "row", 0)
    column = blocks[:, :, 0, :].reshape(row_tiles * front_width, front_width)
    solved = jax.scipy.linalg.solve_triangular(factor, column.T, lower=True).T.reshape(
        row_tiles, front_width, front_width
    )
    tile_index = lax.broadcasted_iota(jnp.int32, (row_tiles, 1, 1), 0) * row_size + my_row
    kept = jnp.where(tile_index == 0, factor[None, :, :], solved)
    below = jnp.where(tile_index == 0, 0.0, solved)
    row_panel = broadcast(below, "col", 0)
    group = col_size // row_size
    whole = lax.all_gather(row_panel, "row", axis=0, tiled=True)
    whole = whole.reshape(row_size, col_tiles, group, front_width, front_width)
    picked = lax.dynamic_index_in_dim(whole, my_col % row_size, 0, keepdims=False)
    col_panel = lax.dynamic_index_in_dim(picked, my_col // row_size, 1, keepdims=False)
    blocks = blocks - jnp.einsum("asx,bqx->asbq", row_panel, col_panel, precision=largest_index)
    first_column = jnp.where(my_col == 0, kept, blocks[:, :, 0, :])
    blocks = blocks.at[:, :, 0, :].set(first_column)
    blocks = jnp.where(tile_i >= tile_j, blocks, 0.0)
    return blocks.reshape(row_tiles, 1, front_width, col_tiles, 1, front_width)


def solution(mesh):
    return jax.shard_map(
        on_device,
        mesh=mesh,
        in_specs=(
            P(None, "row", "col", None, None, None),
            P("row", "col", None, None, None),
            P("row", "col", None),
            P("row", "col", None),
            P("row", "col"),
            P("row", "col", None, None),
            P("row", "col", None, None),
        ),
        out_specs=P(None, "row", None, None, "col", None),
        check_vma=False,
    )
```

profile of v0, /device:TPU:0, one launch (start us, length us, event | category | flops | bytes accessed | tf_op | source)
XLA Modules:
  0.0 1470.2 jit_solution(9605571834959242759)
XLA Ops:
  15.7 4.1 fusion.33
  19.8 4.2 all-to-all-start.1
  24.0 30.6 %copy.67 = f32[16,1,32,8,8,256]{5,3,2,0,1,4:T(8,128)} copy(f32[16,1,32,8,8,256]{5,4,3,2,1,0:T(8,128)} %param.9) | data formatting | bytes 67108864 | tf_op args[0]
  55.9 7.1 all-to-all-start
  64.2 5.8 all-reduce.1
  70.0 5.0 all_gather.14
  75.0 5.2 all_gather.17
  84.8 30.9 %convolution_bitcast_fusion = f32[256,256,16,8]{1,2,3,0:T(8,128)} fusion(f32[4,2,256,256,1]{3,2,1,0,4:T(8,128)S(1)} %bitcast.110, f32[16,8,4,2]{0,1,3,2:T(8,128)S(1)} %convolution_bitcast_fusion.1), kind=kOutput, calls=%fused_computation.8 | convolution fusion | flops 805306368 | bytes 35655680 | tf_op jit(solution)/shard_map/absp,spxy->axby/dot_general | solution.py:95
  115.7 34.4 %copy.72 = f32[256,256,16,8]{0,1,3,2:T(8,128)} copy(f32[256,256,16,8]{1,2,3,0:T(8,128)} %convolution_bitcast_fusion) | data formatting | bytes 67108864 | tf_op jit(solution)/shard_map/absp,spxy->axby/dot_general | solution.py:95
  150.2 637.7 %all-to-all-done = f32[16,1,32,8,8,256]{5,3,2,0,1,4:T(8,128)} async-done(((f32[16,1,32,8,8,256]{5,3,2,0,1,4:T(8,128)}), f32[16,1,32,8,8,256]{5,3,2,0,1,4:T(8,128)}, u32[]{:S(2)}, u32[]{:S(2)}) %all-to-all-start) | async-done | bytes 33554464 | tf_op jit(solution)/shard_map/all_to_all | solution.py:30
  787.9 22.9 %copy.68 = f32[16,1,32,8,8,256]{5,3,2,4,0,1:T(8,128)} copy(f32[16,1,32,8,8,256]{5,3,2,0,1,4:T(8,128)} %all-to-all-done) | data formatting | bytes 67108864 | tf_op jit(solution)/shard_map/all_to_all | solution.py:30
  810.7 35.0 %copy.73 = f32[16,256,8,256]{1,3,2,0:T(8,128)} copy(f32[16,256,8,256]{3,2,1,0:T(8,128)} %bitcast.104) | data formatting | bytes 67108864 | tf_op jit(solution)/shard_map/reshape | solution.py:33
  845.7 33.5 %bitcast_add_fusion.1 = f32[16,256,8,256]{1,3,2,0:T(8,128)} fusion(f32[16,256,8,256]{1,3,2,0:T(8,128)} %copy.73, f32[256,256,16,8]{0,1,3,2:T(8,128)} %copy.72), kind=kLoop, calls=%fused_computation.5 | loop fusion | flops 8388608 | bytes 100663296 | tf_op jit(solution)/shard_map/add | solution.py:95
  879.2 31.9 %copy.74 = f32[16,256,8,256]{3,1,2,0:T(8,128)} copy(f32[16,256,8,256]{1,3,2,0:T(8,128)} %bitcast_add_fusion.1) | data formatting | bytes 67108864 | tf_op jit(solution)/shard_map/add | solution.py:95
  911.2 33.6 %fusion.1 = f32[16,256,8,256]{1,3,2,0:T(8,128)} fusion(f32[16,256,8,256]{1,3,2,0:T(8,128)} %bitcast_add_fusion.1, f32[16,256,8,256]{3,1,2,0:T(8,128)} %copy.74, pred[16,8]{1,0:T(8,128)(4,1)S(1)} %get-tuple-element.42), kind=kLoop, calls=%fused_computation.4 | loop fusion | flops 25165824 | bytes 100663424 | tf_op jit(solution)/shard_map/jit(_where)/select_n | solution.py:99
  947.0 11.7 cholesky.50
  958.7 9.8 custom-call.15
  969.0 11.7 cholesky.105
  983.6 4.5 slice.96
  988.1 5.8 copy.76
  993.9 5.7 copy.77
  999.6 14.6 all-reduce.5.cloned.1.call-done
  1019.0 19.7 %custom-call.16 = f32[2,128,128]{1,2,0:T(8,128)S(1)} custom-call(f32[2,128,128]{2,1,0:T(8,128)S(1)} %get-tuple-element.24), custom_call_target="InvertDiagBlocksLowerTriangular" | custom-call | tf_op jit(solution)/shard_map/jit(_solve_triangular)/triangular_solve | solution.py:106
  1048.6 5.6 copy.94
  1054.2 4.7 select_select_fusion
  1059.0 156.4 %all-reduce.7.cloned.1.call-done = f32[16,256,256]{2,1,0:T(8,128)} async-done(((f32[16,256,256]{2,1,0:T(8,128)}), f32[16,256,256]{2,1,0:T(8,128)}) %all-reduce.7.cloned.1.call-update) | async-done | bytes 4194320 | tf_op jit(solution)/shard_map/psum | solution.py:9
  1215.5 5.6 copy.83
  1221.2 100.9 %all-gather.2.cloned.1.call-done = f32[64,256,256]{2,1,0:T(8,128)} async-done(((f32[16,256,256]{2,1,0:T(8,128)}), f32[64,256,256]{2,1,0:T(8,128)}) %all-gather.2.cloned.1.call-update) | async-done | bytes 16777232 | tf_op jit(solution)/shard_map/all_gather | solution.py:114
  1322.0 35.3 %convolution_subtract_fusion = f32[16,256,8,256]{1,3,2,0:T(8,128)} fusion(f32[16,256,8,256]{1,3,2,0:T(8,128)} %fusion.1, f32[16,256,256]{2,1,0:T(8,128)} %all-reduce.7.cloned.1.call-done, f32[4,8,2,256,256]{4,3,2,1,0:T(8,128)} %bitcast.111, s32[]{:T(128)S(6)} %select_n.139, s32[]{:T(128)S(6)} %select_n.142), kind=kOutput, calls=%fused_computation.7 | convolution fusion | flops 25778192384 | bytes 73400328 | tf_op jit(solution)/shard_map/asx,bqx->asbq/dot_general | solution.py:118
  1357.3 4.8 fusion.2
  1362.2 22.9 %select_bitcast_fusion = f32[16,1,256,8,1,256]{2,5,3,0,4,1:T(8,128)} fusion(f32[16,256,8,256]{1,3,2,0:T(8,128)} %fusion.2, pred[16,8]{1,0:T(8,128)(4,1)S(1)} %copy-done.6), kind=kLoop, calls=%fused_computation.6 | loop fusion | flops 8388608 | bytes 67108992 | tf_op jit(solution)/shard_map/reshape | solution.py:122
  1385.1 78.3 %copy.84 = f32[16,1,256,8,1,256]{5,4,3,2,1,0:T(1,128)} copy(f32[16,1,256,8,1,256]{2,5,3,0,4,1:T(8,128)} %select_bitcast_fusion) | data formatting | bytes 67108864 | tf_op jit(solution)/shard_map/reshape | solution.py:122
  (80 shorter events, 38.6 us)
Async XLA Ops:
  6.5 1.6 copy-start
  6.5 3.8 copy-start.7
  19.8 34.8 %all-to-all-start.1 = ((f32[4,2,65536]{2,1,0:T(2,128)}), f32[4,2,65536]{2,1,0:T(2,128)S(1)}, u32[]{:S(2)}, u32[]{:S(2)}) async-start(f32[4,2,65536]{2,1,0:T(2,128)} %fusion.33), calls=%async_computation.1 | async-start | bytes 4194304 | tf_op jit(solution)/shard_map/all_to_all | solution.py:69
  54.6 8.5 copy-start.10
  54.6 15.4 %copy-start.8 = (s32[1,1,8]{2,1,0:T(1,128)S(1)}, s32[1,1,8]{2,1,0:T(1,128)}, u32[]{:S(2)}) copy-start(s32[1,1,8]{2,1,0:T(1,128)} %param.11) | copy-start | bytes 100
  54.6 20.5 %copy-start.9 = (s32[1,1,8]{2,1,0:T(1,128)S(1)}, s32[1,1,8]{2,1,0:T(1,128)}, u32[]{:S(2)}) copy-start(s32[1,1,8]{2,1,0:T(1,128)} %param.12) | copy-start | bytes 100
  54.6 1.3 copy-start.4
  55.9 731.9 %all-to-all-start = ((f32[16,1,32,8,8,256]{5,3,2,0,1,4:T(8,128)}), f32[16,1,32,8,8,256]{5,3,2,0,1,4:T(8,128)}, u32[]{:S(2)}, u32[]{:S(2)}) async-start(f32[16,1,32,8,8,256]{5,3,2,0,1,4:T(8,128)} %copy.67), calls=%async_computation | async-start | bytes 67108864 | tf_op jit(solution)/shard_map/all_to_all | solution.py:30
  63.0 951.1 %all-reduce.5.cloned.1.call-start = ((), (), s32[]{:S(2)}) async-start(), calls=%async_computation.2 | async-start | bytes 524288 | tf_op jit(solution)/shard_map/psum | solution.py:9
  983.5 231.9 %all-reduce.7.cloned.1.call-start = ((), (), s32[]{:S(2)}) async-start(), calls=%async_computation.3 | async-start | bytes 8388608 | tf_op jit(solution)/shard_map/psum | solution.py:9
  1038.7 3.7 copy-start.3
  1059.0 263.1 %all-gather.2.cloned.1.call-start = ((), (), s32[]{:S(2)}) async-start(), calls=%async_computation.4 | async-start | bytes 20971520 | tf_op jit(solution)/shard_map/all_gather | solution.py:114
  1215.5 5.6 copy-start.5
  1322.0 35.3 %copy-start.2 = (f32[16,256,1,256]{1,3,2,0:T(8,128)S(1)}, f32[16,256,1,256]{1,3,2,0:T(8,128)}, u32[]{:S(2)}) copy-start(f32[16,256,1,256]{1,3,2,0:T(8,128)} %copy.83) | copy-start | bytes 12582916
  1357.3 4.8 copy-start.6
  1385.1 78.3 %copy-start.1 = (f32[1,1,8,256,256]{4,3,2,1,0:T(8,128)S(1)}, f32[1,1,8,256,256]{4,3,2,1,0:T(8,128)}, u32[]{:S(2)}) copy-start(f32[1,1,8,256,256]{4,3,2,1,0:T(8,128)} %param.10) | copy-start | bytes 6291460
Sparse Core Ops, SparseCore 0:
  983.6 30.4 all-reduce.4
  1059.1 156.2 all-reduce.6
  1217.1 104.9 all-gather.1
where the time goes:
time: 1480 us; the launch traced here: 1470 us
  waiting for transfers between devices  910 us (61%)
  local copies, waits for them, and re-layouts  273 us (18%)
  other arithmetic  162 us (11%)
  matrix products  83.3 us (6%)
  blocking collectives  16 us (1%)
  between operations  15.5 us (1%)
    all_to_all x1, waiting for transfers between devices, on_device(): lax.all_to_all(front_panels, 'col', split_axis=4, concat_axis=2, tiled=True)  638 us
    psum x2, waiting for transfers between devices, broadcast(): return lax.psum(kept, axis)  171 us
    all_gather x1, waiting for transfers between devices, on_device(): whole = lax.all_gather(row_panel, 'row', axis=0, tiled=True)  101 us
    reshape x1, local copies, waits for them, and re-layouts, on_device(): return blocks.reshape(row_tiles, 1, front_width, col_tiles, 1, front_width)  78.3 us
    dot_general x1, matrix products, on_device(): jnp.einsum('asx,bqx->asbq', row_panel, col_panel, precision=largest_index)  35.3 us
    reshape x1, local copies, waits for them, and re-layouts, on_device(): blocks = blocks.reshape(row_tiles, front_width, col_tiles, front_width)  35 us
    dot_general x1, local copies, waits for them, and re-layouts, on_device(): jnp.einsum('absp,spxy->axby', landing, incoming, precision=largest_index)  34.4 us
    another operation x6, other arithmetic, on_device(): factor = jnp.linalg.cholesky(jnp.where(at_root, corner, identity))  34 us
  transfers between devices with their start and end apart: 5, of which 4 were waited for; matrix products, arithmetic and copies ran while one was open for 8% of the time, Pallas kernels for 0%

commit v1 on v0

--- a/solution.py
+++ b/solution.py
@@ -6,7 +6,11 @@
 
 def broadcast(value, axis, source):
     kept = jnp.where(lax.axis_index(axis) == source, value, 0).astype(value.dtype)
-    return lax.psum(kept, axis)
+
+    def arrange_column(arr_in):
+        return jnp.sum(lax.all_gather(arr_in, axis), axis=0)
+
+    return arrange_column(kept)
 
 
 def slot_positions(owners, is_live):

time: 1480 us -> 1960 us (1.32)
  waiting for transfers between devices: 910 us -> 1370 us
    all_gather x0 -> x2, waiting for transfers between devices: none -> 637 us  [arrange_column(): return jnp.sum(lax.all_gather(arr_in, axis), axis=0)]
    psum x2 -> x0, waiting for transfers between devices: 171 us -> none  [broadcast(): return lax.psum(kept, axis)]
    unnamed x26 -> x25, local copies, waits for them, and re-layouts: 33.2 us -> 39.3 us
  transfers between devices with their start and end apart: 5 -> 5, of which waited for: 4 -> 3; matrix products, arithmetic and copies ran while one was open for 8% -> 7% of each run, Pallas kernels for 0% -> 0%
where the time goes in v1:
time: 1960 us; the launch traced here: 1950 us
  waiting for transfers between devices  1370 us (70%)
  local copies, waits for them, and re-layouts  279 us (14%)
  other arithmetic  177 us (9%)
  matrix products  83.7 us (4%)
    all_to_all x1, waiting for transfers between devices, on_device(): lax.all_to_all(front_panels, 'col', split_axis=4, concat_axis=2, tiled=True)  637 us
    all_gather x2, waiting for transfers between devices, arrange_column(): return jnp.sum(lax.all_gather(arr_in, axis), axis=0)  637 us
    all_gather x1, waiting for transfers between devices, on_device(): whole = lax.all_gather(row_panel, 'row', axis=0, tiled=True)  94.7 us
    reshape x1, local copies, waits for them, and re-layouts, on_device(): return blocks.reshape(row_tiles, 1, front_width, col_tiles, 1, front_width)  78.3 us
    unnamed x25, local copies, waits for them, and re-layouts  39.3 us
  transfers between devices with their start and end apart: 5, of which 3 were waited for; matrix products, arithmetic and copies ran while one was open for 7% of the time, Pallas kernels for 0%

profile of v1, /device:TPU:0, one launch (start us, length us, event | category | flops | bytes accessed | tf_op | source)
XLA Modules:
  0.0 1951.1 jit_solution(7079363778250343675)
XLA Ops:
  19.8 4.2 all-to-all-start.1
  24.0 30.6 %copy.71 = f32[16,1,32,8,8,256]{5,3,2,0,1,4:T(8,128)} copy(f32[16,1,32,8,8,256]{5,4,3,2,1,0:T(8,128)} %param.9) | data formatting | bytes 67108864 | tf_op args[0]
  55.9 7.1 all-to-all-start
  64.4 5.8 all-reduce.1
  70.2 5.0 all_gather.24
  75.3 5.2 all_gather.27
  85.0 30.9 %convolution_bitcast_fusion = f32[256,256,16,8]{1,2,3,0:T(8,128)} fusion(f32[4,2,256,256,1]{3,2,1,0,4:T(8,128)S(1)} %bitcast.108, f32[16,8,4,2]{0,1,3,2:T(8,128)S(1)} %convolution_bitcast_fusion.1), kind=kOutput, calls=%fused_computation.8 | convolution fusion | flops 805306368 | bytes 35655680 | tf_op jit(solution)/shard_map/absp,spxy->axby/dot_general | solution.py:99
  116.0 34.4 %copy.76 = f32[256,256,16,8]{0,1,3,2:T(8,128)} copy(f32[256,256,16,8]{1,2,3,0:T(8,128)} %convolution_bitcast_fusion) | data formatting | bytes 67108864 | tf_op jit(solution)/shard_map/absp,spxy->axby/dot_general | solution.py:99
  150.4 637.4 %all-to-all-done = f32[16,1,32,8,8,256]{5,3,2,0,1,4:T(8,128)} async-done(((f32[16,1,32,8,8,256]{5,3,2,0,1,4:T(8,128)}), f32[16,1,32,8,8,256]{5,3,2,0,1,4:T(8,128)}, u32[]{:S(2)}, u32[]{:S(2)}) %all-to-all-start) | async-done | bytes 33554464 | tf_op jit(solution)/shard_map/all_to_all | solution.py:34
  787.8 22.9 %copy.72 = f32[16,1,32,8,8,256]{5,3,2,4,0,1:T(8,128)} copy(f32[16,1,32,8,8,256]{5,3,2,0,1,4:T(8,128)} %all-to-all-done) | data formatting | bytes 67108864 | tf_op jit(solution)/shard_map/all_to_all | solution.py:34
  810.7 35.0 %copy.77 = f32[16,256,8,256]{1,3,2,0:T(8,128)} copy(f32[16,256,8,256]{3,2,1,0:T(8,128)} %bitcast.101) | data formatting | bytes 67108864 | tf_op jit(solution)/shard_map/reshape | solution.py:37
  845.7 33.5 %bitcast_add_fusion.1 = f32[16,256,8,256]{1,3,2,0:T(8,128)} fusion(f32[16,256,8,256]{1,3,2,0:T(8,128)} %copy.77, f32[256,256,16,8]{0,1,3,2:T(8,128)} %copy.76), kind=kLoop, calls=%fused_computation.5 | loop fusion | flops 8388608 | bytes 100663296 | tf_op jit(solution)/shard_map/add | solution.py:99
  879.2 31.9 %copy.78 = f32[16,256,8,256]{3,1,2,0:T(8,128)} copy(f32[16,256,8,256]{1,3,2,0:T(8,128)} %bitcast_add_fusion.1) | data formatting | bytes 67108864 | tf_op jit(solution)/shard_map/add | solution.py:99
  911.2 33.6 %fusion.1 = f32[16,256,8,256]{1,3,2,0:T(8,128)} fusion(f32[16,256,8,256]{1,3,2,0:T(8,128)} %bitcast_add_fusion.1, f32[16,256,8,256]{3,1,2,0:T(8,128)} %copy.78, pred[16,8]{1,0:T(8,128)(4,1)S(1)} %get-tuple-element.42), kind=kLoop, calls=%fused_computation.4 | loop fusion | flops 25165824 | bytes 100663424 | tf_op jit(solution)/shard_map/jit(_where)/select_n | solution.py:103
  946.9 11.7 cholesky.50
  958.7 9.8 custom-call.15
  969.0 11.7 cholesky.105
  983.6 4.5 slice.96
  988.1 5.8 copy.80
  993.9 5.6 copy.81
  1004.9 19.7 %custom-call.16 = f32[2,128,128]{1,2,0:T(8,128)S(1)} custom-call(f32[2,128,128]{2,1,0:T(8,128)S(1)} %get-tuple-element.24), custom_call_target="InvertDiagBlocksLowerTriangular" | custom-call | tf_op jit(solution)/shard_map/jit(_solve_triangular)/triangular_solve | solution.py:110
  1034.5 5.6 copy.101
  1040.1 4.7 select_select_fusion
  1044.9 637.1 %all-gather.5.cloned.1.call-done = f32[8,16,256,256]{3,2,1,0:T(8,128)} async-done(((f32[1,16,256,256]{3,2,1,0:T(8,128)}), f32[8,16,256,256]{3,2,1,0:T(8,128)}) %all-gather.5.cloned.1.call-update) | async-done | bytes 33554448 | tf_op jit(solution)/shard_map/all_gather | solution.py:11
  1682.0 14.4 reduce_sum.39
  1696.6 5.4 copy.90
  1702.0 5.9 copy.104
  1707.9 94.7 %all-gather.7.cloned.1.call-done = f32[64,256,256]{2,1,0:T(8,128)} async-done(((f32[16,256,256]{2,1,0:T(8,128)}), f32[64,256,256]{2,1,0:T(8,128)}) %all-gather.7.cloned.1.call-update) | async-done | bytes 16777232 | tf_op jit(solution)/shard_map/all_gather | solution.py:118
  1802.5 35.7 %convolution_subtract_fusion = f32[16,256,8,256]{1,3,2,0:T(8,128)} fusion(f32[16,256,8,256]{1,3,2,0:T(8,128)} %fusion.1, f32[16,256,256,1]{1,0,2,3:T(8,128)} %bitcast.104, f32[4,8,2,256,256]{4,3,2,1,0:T(8,128)} %bitcast.110, s32[]{:T(128)S(6)} %select_n.153, s32[]{:T(128)S(6)} %select_n.156), kind=kOutput, calls=%fused_computation.7 | convolution fusion | flops 25778192384 | bytes 73400328 | tf_op jit(solution)/shard_map/asx,bqx->asbq/dot_general | solution.py:122
  1838.3 4.8 fusion.2
  1843.1 22.9 %select_bitcast_fusion = f32[16,1,256,8,1,256]{2,5,3,0,4,1:T(8,128)} fusion(f32[16,256,8,256]{1,3,2,0:T(8,128)} %fusion.2, pred[16,8]{1,0:T(8,128)(4,1)S(1)} %copy-done.5), kind=kLoop, calls=%fused_computation.6 | loop fusion | flops 8388608 | bytes 67108992 | tf_op jit(solution)/shard_map/reshape | solution.py:126
  1866.0 78.3 %copy.91 = f32[16,1,256,8,1,256]{5,4,3,2,1,0:T(1,128)} copy(f32[16,1,256,8,1,256]{2,5,3,0,4,1:T(8,128)} %select_bitcast_fusion) | data formatting | bytes 67108864 | tf_op jit(solution)/shard_map/reshape | solution.py:126
  (81 shorter events, 43.3 us)
Async XLA Ops:
  6.5 1.6 copy-start
  6.5 3.8 copy-start.6
  19.8 34.8 %all-to-all-start.1 = ((f32[4,2,65536]{2,1,0:T(2,128)}), f32[4,2,65536]{2,1,0:T(2,128)S(1)}, u32[]{:S(2)}, u32[]{:S(2)}) async-start(f32[4,2,65536]{2,1,0:T(2,128)} %fusion.33), calls=%async_computation.1 | async-start | bytes 4194304 | tf_op jit(solution)/shard_map/all_to_all | solution.py:73
  54.6 8.5 copy-start.9
  54.6 15.7 copy-start.7
  54.6 20.7 %copy-start.8 = (s32[1,1,8]{2,1,0:T(1,128)S(1)}, s32[1,1,8]{2,1,0:T(1,128)}, u32[]{:S(2)}) copy-start(s32[1,1,8]{2,1,0:T(1,128)} %param.12) | copy-start | bytes 100
  54.6 1.3 copy-start.4
  55.9 731.9 %all-to-all-start = ((f32[16,1,32,8,8,256]{5,3,2,0,1,4:T(8,128)}), f32[16,1,32,8,8,256]{5,3,2,0,1,4:T(8,128)}, u32[]{:S(2)}, u32[]{:S(2)}) async-start(f32[16,1,32,8,8,256]{5,3,2,0,1,4:T(8,128)} %copy.71), calls=%async_computation | async-start | bytes 67108864 | tf_op jit(solution)/shard_map/all_to_all | solution.py:34
  63.0 936.6 %all-gather.9.cloned.1.call-start = ((), (), s32[]{:S(2)}) async-start(), calls=%async_computation.4 | async-start | bytes 1310720 | tf_op jit(solution)/shard_map/all_gather | solution.py:11
  983.5 698.5 %all-gather.5.cloned.1.call-start = ((), (), s32[]{:S(2)}) async-start(), calls=%async_computation.2 | async-start | bytes 37748736 | tf_op jit(solution)/shard_map/all_gather | solution.py:11
  1024.6 3.7 copy-start.3
  1044.8 757.7 %all-gather.7.cloned.1.call-start = ((), (), s32[]{:S(2)}) async-start(), calls=%async_computation.3 | async-start | bytes 20971520 | tf_op jit(solution)/shard_map/all_gather | solution.py:118
  1802.5 35.7 %copy-start.2 = (f32[16,256,1,256]{1,3,2,0:T(8,128)S(1)}, f32[16,256,1,256]{1,3,2,0:T(8,128)}, u32[]{:S(2)}) copy-start(f32[16,256,1,256]{1,3,2,0:T(8,128)} %copy.90) | copy-start | bytes 12582916
  1838.3 4.8 copy-start.5
  1866.0 78.3 %copy-start.1 = (f32[1,1,8,256,256]{4,3,2,1,0:T(8,128)S(1)}, f32[1,1,8,256,256]{4,3,2,1,0:T(8,128)}, u32[]{:S(2)}) copy-start(f32[1,1,8,256,256]{4,3,2,1,0:T(8,128)} %param.10) | copy-start | bytes 6291460
Sparse Core Ops, SparseCore 0:
  983.6 15.1 all-gather.8
  1045.0 637.0 all-gather.4
  1696.6 105.8 all-gather.6
